TPU v7x, 512 devices: a whole 4x4x16 slice. The times are simulated.
512 devices in a mesh: img: 32 (over x, z_hi, core), py: 4 (over y), px: 4 (over z_lo).
Axes of the slice: x: 4, y: 4, z: 16 (z_hi: 4, z_lo: 4; z = z_hi * 4 + z_lo), core: 2. Of those that a mesh axis runs over, the one named last changes fastest.
Arguments:
- queries: bfloat16 [32, 64, 64, 1536], P('img', 'py', 'px')
- keys: bfloat16 [32, 64, 64, 1536], P('img', 'py', 'px')
- values: bfloat16 [32, 64, 64, 1536], P('img', 'py', 'px'), may hold values from -6 to 6
- pattern: int32 [32, 8, 8, 9], P('img', 'py', 'px'), may hold values from 0 to 1, as said below
- targets: int32 [32, 8, 8, 12, 3], P('img', 'py', 'px'), may hold values from 0 to 8, as said below
- router_q: float32 [12, 128, 64], replicated, may hold values from -1.5 to 1.5
- router_k: float32 [12, 128, 64], replicated, may hold values from -1.5 to 1.5
Outputs:
- attended: bfloat16 [32, 64, 64, 1536], P('img', 'py', 'px')
- grad_q: float32 [12, 128, 64], replicated
- grad_k: float32 [12, 128, 64], replicated
Inputs may be any that keep to these rules, and one draw needn't show every extreme that they name: `pattern`: the centre offset and the offsets one block away along one axis that lie in the image are 1; offsets outside the image are 0. `targets`: 3 different offsets per query block and head, each with pattern 1.
All inputs are finite; a program needn't handle non-finite values.
Results may differ from a plain program's by a relative error of at most 0.0049.
Values may be sent and summed in bfloat16 or wider, within the bound.
No kernel may reach another device: no remote copies, remote signals or barrier semaphores. Data moves between devices by JAX's collectives and lax.ppermute only.
A program may use at most 64 MiB of HBM per device.

v0:
```python
import math
import jax
import jax.numpy as jnp
from jax import lax
from jax.sharding import PartitionSpec as P

HEADS = 12
DH = 128
RW = 64
BS = 8
RADIUS = 1
TOPK = 3
NOFF = 9


def extended_2(cells, sides, width):
    for axis, dim in sides:
        count = lax.axis_size(axis)
        ends = count - 1
        head = lax.slice_in_dim(cells, 0, width, axis=dim)
        tail = lax.slice_in_dim(cells, cells.shape[dim] - width, cells.shape[dim], axis=dim)
        cells = jnp.concatenate(
            [
                lax.ppermute(tail, axis, [(i, (i + 1) % count) for i in range(ends)]),
                cells,
                lax.ppermute(head, axis, [((i + 1) % count, i) for i in range(ends)]),
            ],
            axis=dim,
        )
    return cells


def attend(query_tile, key_ext, value_ext, live):
    tile_y, tile_x, feat = query_tile.shape
    blocks_y = tile_y // BS
    blocks_x = tile_x // BS
    width = 2 * RADIUS + 1
    side = width * BS
    scale = 1.0 / math.sqrt(DH)
    anchor = jnp.zeros((), jnp.int32)

    def regroup(window):
        return (
            window.reshape(width, BS, width, BS, feat)
            .transpose(0, 2, 1, 3, 4)
            .reshape(NOFF * BS * BS, HEADS, DH)
        )

    def one_block(index):
        row = index // blocks_x
        col = index % blocks_x
        start_y = row * BS
        start_x = col * BS
        query = lax.dynamic_slice(query_tile, (start_y, start_x, anchor), (BS, BS, feat)).reshape(
            BS * BS, HEADS, DH
        )
        window_k = regroup(
            lax.dynamic_slice(key_ext, (start_y, start_x, anchor), (side, side, feat))
        )
        window_v = regroup(
            lax.dynamic_slice(value_ext, (start_y, start_x, anchor), (side, side, feat))
        )
        mask_row = lax.dynamic_slice(live, (row, col, anchor), (1, 1, NOFF)).reshape(NOFF)
        key_mask = jnp.repeat(mask_row, BS * BS) > 0
        scores = (
            jnp.einsum("qhd,khd->hqk", query, window_k, preferred_element_type=jnp.float32) * scale
        )
        scores = jnp.where(key_mask[None, None, :], scores, -1e30)
        top = jnp.max(scores, axis=-1, keepdims=True)
        weights = jnp.exp(scores - top)
        probs = (weights / jnp.sum(weights, axis=-1, keepdims=True)).astype(jnp.bfloat16)
        out = jnp.einsum("hqk,khd->qhd", probs, window_v, preferred_element_type=jnp.float32)
        return out.astype(jnp.bfloat16).reshape(BS, BS, feat)

    outs = lax.map(one_block, jnp.arange(blocks_y * blocks_x, dtype=jnp.int32))
    return (
        outs.reshape(blocks_y, blocks_x, BS, BS, feat)
        .transpose(0, 2, 1, 3, 4)
        .reshape(tile_y, tile_x, feat)
    )


def pooling(tile):
    tile_y, tile_x, feat = tile.shape
    shaped = tile.reshape(tile_y // BS, BS, tile_x // BS, BS, HEADS, DH)
    return jnp.sum(shaped, axis=(1, 3), dtype=jnp.float32) / (BS * BS)


def router_loss(weights_q, weights_k, pooled_q, pooled_k, live, chosen):
    route_q = jnp.einsum("yxhd,hdr->yxhr", pooled_q, weights_q, precision=lax.Precision.HIGHEST)
    route_k = jnp.einsum("yxhd,hdr->yxhr", pooled_k, weights_k, precision=lax.Precision.HIGHEST)
    blocks_y, blocks_x = (pooled_q.shape[0], pooled_q.shape[1])
    width = 2 * RADIUS + 1
    shifted = jnp.stack(
        [
            route_k[up : up + blocks_y, left : left + blocks_x]
            for up in range(width)
            for left in range(width)
        ],
        axis=2,
    )
    logits = jnp.einsum(
        "yxhr,yxohr->yxho", route_q, shifted, precision=lax.Precision.HIGHEST
    ) / math.sqrt(RW)
    logits = jnp.where(live[:, :, None, :] > 0, logits, -1e30)
    top = jnp.max(logits, axis=-1, keepdims=True)
    logz = top + jnp.log(jnp.sum(jnp.exp(logits - top), axis=-1, keepdims=True))
    logp = logits - logz
    picks = (chosen[..., None] == jnp.arange(NOFF, dtype=jnp.int32)).astype(jnp.float32)
    return -jnp.sum(picks * logp[:, :, :, None, :])


def per_device(queries, keys, values, pattern, targets, router_q, router_k):
    rim = RADIUS * BS
    stacked = jnp.stack([keys, values])
    extended = extended_2(stacked, (("py", 2), ("px", 3)), rim)
    key_ext = extended[0, 0]
    value_ext = extended[1, 0]
    attended = attend(queries[0], key_ext, value_ext, pattern[0])[None]
    pooled_q = pooling(queries[0])
    pooled_k = pooling(key_ext)
    blocks_y = pooled_q.shape[0]
    blocks_x = pooled_q.shape[1]
    normal = float(TOPK * HEADS * blocks_y * lax.axis_size("py") * blocks_x * lax.axis_size("px"))

    def local_loss(weights_q, weights_k):
        return (
            router_loss(weights_q, weights_k, pooled_q, pooled_k, pattern[0], targets[0]) / normal
        )

    grad_q, grad_k = jax.grad(local_loss, argnums=(0, 1))(router_q, router_k)
    grad_q, grad_k = lax.psum((grad_q, grad_k), ("img", "py", "px"))
    return (attended, grad_q, grad_k)


def solution(mesh):
    return jax.shard_map(
        per_device,
        mesh=mesh,
        in_specs=(
            P("img", "py", "px", None),
            P("img", "py", "px", None),
            P("img", "py", "px", None),
            P("img", "py", "px", None),
            P("img", "py", "px", None, None),
            P(),
            P(),
        ),
        out_specs=(P("img", "py", "px", None), P(), P()),
        check_vma=False,
    )
```

profile of v0, /device:TPU:2, one launch (start us, length us, event | category | flops | bytes accessed | tf_op | source)
XLA Modules:
  0.0 595.2 jit_solution(9057163803612186937)
XLA Ops:
  7.2 1.6 fusion.31
  8.9 3.5 collective-permute-start
  13.7 15.4 %collective-permute-done = bf16[2,1,8,16,1536]{4,3,2,1,0:T(8,128)(2,1)S(1)} collective-permute-done((bf16[2,1,8,16,1536]{4,3,2,1,0:T(8,128)(2,1)S(1)}, bf16[2,1,8,16,1536]{4,3,2,1,0:T(8,128)(2,1)S(1)}, u32[]{:S(2)}, u32[]{:S(2)}) %collective-permute-start) | collective-permute-done | bytes 786464 | tf_op jit(solution)/shard_map/ppermute | solution.py:24
  29.1 4.2 collective-permute-done.1
  34.6 1.9 fusion.85
  36.5 5.0 collective-permute-start.2
  44.5 1.7 fusion.37
  46.2 26.9 %collective-permute-done.2 = bf16[2,1,32,8,1536]{4,3,2,1,0:T(8,128)(2,1)} collective-permute-done((bf16[2,1,32,8,1536]{4,3,2,1,0:T(8,128)(2,1)}, bf16[2,1,32,8,1536]{4,3,2,1,0:T(8,128)(2,1)}, u32[]{:S(2)}, u32[]{:S(2)}) %collective-permute-start.2) | collective-permute-done | bytes 1572896 | tf_op jit(solution)/shard_map/ppermute | solution.py:24
  73.2 5.3 collective-permute-done.3
  78.5 3.2 pad_maximum_fusion
  81.6 2.4 fusion.84
  93.8 1.6 copy.53
  98.7 1.5 fusion.32
  100.1 2.3 convolution_bitcast_fusion
  102.5 2.6 convolution_bitcast_fusion.1
  105.1 122.5 %while.12 = (s32[]{:T(128)}, bf16[4,8,8,1536]{3,2,1,0:T(8,128)(2,1)}, s32[4]{0:T(128)S(1)}, bf16[32,32,1536]{2,1,0:T(8,128)(2,1)}, s32[2,2,9]{2,1,0:T(2,128)S(1)...) while((s32[]{:T(128)}, ...), condition=%wide.region_3.4_spmd, body=%wide.region_0.3_spmd.sunk | while | flops 343820224 | bytes 57812960 | solution.py:75
  108.5 3.0 constant_dynamic-slice_fusion.6
  111.5 1.5 copy.118
  113.0 3.0 reshape.102
  117.1 2.2 fusion.101
  119.5 2.0 fusion.100
  121.6 1.6 copy.117
  123.2 2.7 reshape.101
  125.9 4.7 fusion.102
  130.6 1.8 copy.119
  132.3 1.8 broadcast_in_dim.131
  134.1 1.6 constant_dynamic-update-slice_fusion.2
  139.1 3.1 constant_dynamic-slice_fusion.6
  142.1 1.5 copy.118
  143.6 3.0 reshape.102
  147.7 2.2 fusion.101
  150.2 2.0 fusion.100
  152.2 1.6 copy.117
  153.8 2.7 reshape.101
  156.5 4.7 fusion.102
  161.2 1.8 copy.119
  163.0 1.8 broadcast_in_dim.131
  164.7 1.6 constant_dynamic-update-slice_fusion.2
  169.7 3.0 constant_dynamic-slice_fusion.6
  172.7 1.5 copy.118
  174.2 3.0 reshape.102
  178.4 2.2 fusion.101
  180.8 2.0 fusion.100
  182.8 1.6 copy.117
  184.4 2.7 reshape.101
  187.1 4.7 fusion.102
  191.8 1.8 copy.119
  193.6 1.8 broadcast_in_dim.131
  195.3 1.6 constant_dynamic-update-slice_fusion.2
  200.3 3.1 constant_dynamic-slice_fusion.6
  203.4 1.5 copy.118
  204.9 3.0 reshape.102
  209.0 2.2 fusion.101
  211.4 2.0 fusion.100
  213.4 1.6 copy.117
  215.1 2.7 reshape.101
  217.8 4.7 fusion.102
  222.5 1.8 copy.119
  224.2 1.8 broadcast_in_dim.131
  226.0 1.6 constant_dynamic-update-slice_fusion.2
  227.6 2.1 copy.48
  229.7 355.1 %all-reduce.12.cloned.1.call-done = (f32[12,128,64]{1,2,0:T(8,128)}, f32[12,128,64]{1,2,0:T(8,128)}) async-done(((f32[12,128,64]{1,2,0:T(8,128)}, f32[12,128,64]{1,2,0:T(8,128)}), (f32[12,128,64]{1,2,0:T(8,128)}, f32[12,128,64]{1,2,0:T(8,128)})) %all-reduce.12.cloned.1.call-update) | async-done | bytes 786448 | tf_op jit(solution)/shard_map/psum | solution.py:132
  584.8 1.8 copy.137
  586.6 1.8 copy.138
  (95 shorter events, 26.4 us)
Async XLA Ops:
  7.2 78.1 %copy-start = (f32[12,128,64]{1,2,0:T(8,128)S(1)}, f32[12,128,64]{1,2,0:T(8,128)}, u32[]{:S(2)}) copy-start(f32[12,128,64]{1,2,0:T(8,128)} %param.15) | copy-start | bytes 1179652
  7.2 27.0 %copy-start.3 = (bf16[1,16,16,1536]{3,2,1,0:T(8,128)(2,1)S(1)}, bf16[1,16,16,1536]{3,2,1,0:T(8,128)(2,1)}, u32[]{:S(2)}) copy-start(bf16[1,16,16,1536]{3,2,1,0:T(8,128)(2,1)} %param.10) | copy-start | bytes 2359300
  7.2 27.0 %copy-start.4 = (bf16[1,16,16,1536]{3,2,1,0:T(8,128)(2,1)S(1)}, bf16[1,16,16,1536]{3,2,1,0:T(8,128)(2,1)}, u32[]{:S(2)}) copy-start(bf16[1,16,16,1536]{3,2,1,0:T(8,128)(2,1)} %param.11) | copy-start | bytes 2359300
  7.2 577.6 %all-reduce.12.cloned.1.call-start = ((), (), s32[]{:S(2)}) async-start(), calls=%async_computation | async-start | bytes 1572864 | tf_op jit(solution)/shard_map/psum | solution.py:132
  8.9 20.3 %collective-permute-start = (bf16[2,1,8,16,1536]{4,3,2,1,0:T(8,128)(2,1)S(1)}, bf16[2,1,8,16,1536]{4,3,2,1,0:T(8,128)(2,1)S(1)}, u32[]{:S(2)}, u32[]{:S(2)}) collective-permute-start(bf16[2,1,8,16,1536]{4,3,2,1,0:T(8,128)(2,1)S(1)} %get-tuple-element.123), channel_id=1, source_target_pairs={{0,4},{4,8},{8,12},{1,5},{5,9},{9,13},{2,6},{6,10},{10,14},{3,7},{... | collective-permute-start | bytes 2359304 | tf_op jit(solution)/shard_map/ppermute | solution.py:24
  12.4 20.9 %collective-permute-start.1 = (bf16[2,1,8,16,1536]{4,3,2,1,0:T(8,128)(2,1)S(1)}, bf16[2,1,8,16,1536]{4,3,2,1,0:T(8,128)(2,1)S(1)}, u32[]{:S(2)}, u32[]{:S(2)}) collective-permute-start(bf16[2,1,8,16,1536]{4,3,2,1,0:T(8,128)(2,1)S(1)} %get-tuple-element.124), channel_id=1, source_target_pairs={{4,0},{8,4},{12,8},{5,1},{9,5},{13,9},{6,2},{10,6},{14,10},{7,3},{... | collective-permute-start | bytes 2359304 | tf_op jit(solution)/shard_map/ppermute | solution.py:26
  33.3 0.9 copy-start.6
  34.6 8.2 %copy-start.11 = (s32[1,2,2,9]{3,2,1,0:T(2,128)S(1)}, s32[1,2,2,9]{3,2,1,0:T(2,128)}, u32[]{:S(2)}) copy-start(s32[1,2,2,9]{3,2,1,0:T(2,128)} %param.12) | copy-start | bytes 436
  34.6 9.7 %copy-start.5 = (bf16[1,16,16,1536]{3,2,1,0:T(8,128)(2,1)S(1)}, bf16[1,16,16,1536]{3,2,1,0:T(8,128)(2,1)}, u32[]{:S(2)}) copy-start(bf16[1,16,16,1536]{3,2,1,0:T(8,128)(2,1)} %param.9) | copy-start | bytes 2359300
  36.5 36.6 %collective-permute-start.2 = (bf16[2,1,32,8,1536]{4,3,2,1,0:T(8,128)(2,1)}, bf16[2,1,32,8,1536]{4,3,2,1,0:T(8,128)(2,1)}, u32[]{:S(2)}, u32[]{:S(2)}) collective-permute-start(bf16[2,1,32,8,1536]{4,3,2,1,0:T(8,128)(2,1)} %get-tuple-element.121), channel_id=1, source_target_pairs={{0,1},{1,2},{2,3},{4,5},{5,6},{6,7},{8,9},{9,10},{10,11},{12,13},{... | collective-permute-start | bytes 4718600 | tf_op jit(solution)/shard_map/ppermute | solution.py:24
  41.5 36.9 %collective-permute-start.3 = (bf16[2,1,32,8,1536]{4,3,2,1,0:T(8,128)(2,1)}, bf16[2,1,32,8,1536]{4,3,2,1,0:T(8,128)(2,1)}, u32[]{:S(2)}, u32[]{:S(2)}) collective-permute-start(bf16[2,1,32,8,1536]{4,3,2,1,0:T(8,128)(2,1)} %get-tuple-element.122), channel_id=1, source_target_pairs={{1,0},{2,1},{3,2},{5,4},{6,5},{7,6},{9,8},{10,9},{11,10},{13,12},{... | collective-permute-start | bytes 4718600 | tf_op jit(solution)/shard_map/ppermute | solution.py:26
  44.5 34.0 %copy-start.10 = (f32[2,2,12,128]{3,2,1,0:T(8,128)}, f32[2,2,12,128]{3,2,1,0:T(8,128)S(1)}, u32[]{:S(2)}) copy-start(f32[2,2,12,128]{3,2,1,0:T(8,128)S(1)} %broadcast_multiply_fusion.1) | copy-start | bytes 73732
  46.2 40.1 %copy-start.9 = (f32[12,2,2,64]{3,2,1,0:T(2,128)}, f32[12,2,2,64]{3,2,1,0:T(2,128)S(1)}, u32[]{:S(2)}) copy-start(f32[12,2,2,64]{3,2,1,0:T(2,128)S(1)} %fusion.37) | copy-start | bytes 36868
  84.6 0.7 copy-start.8
  86.3 0.7 copy-start.7
  105.1 6.4 %copy-start.1 = (bf16[32,32,1536]{2,1,0:T(8,128)(2,1)}, bf16[32,32,1536]{2,1,0:T(8,128)(2,1)S(1)}, u32[]{:S(2)}) copy-start(bf16[32,32,1536]{2,1,0:T(8,128)(2,1)S(1)} %get-tuple-element.215) | copy-start | bytes 9437188 | tf_op jit(solution)/shard_map/while
  125.9 9.8 %copy-start.2 = (bf16[32,32,1536]{2,1,0:T(8,128)(2,1)S(1)}, bf16[32,32,1536]{2,1,0:T(8,128)(2,1)}, u32[]{:S(2)}) copy-start(bf16[32,32,1536]{2,1,0:T(8,128)(2,1)} %copy-done.1) | copy-start | bytes 9437188 | tf_op jit(solution)/shard_map/while
  135.7 6.4 %copy-start.1 = (bf16[32,32,1536]{2,1,0:T(8,128)(2,1)}, bf16[32,32,1536]{2,1,0:T(8,128)(2,1)S(1)}, u32[]{:S(2)}) copy-start(bf16[32,32,1536]{2,1,0:T(8,128)(2,1)S(1)} %get-tuple-element.215) | copy-start | bytes 9437188 | tf_op jit(solution)/shard_map/while
  156.5 9.9 %copy-start.2 = (bf16[32,32,1536]{2,1,0:T(8,128)(2,1)S(1)}, bf16[32,32,1536]{2,1,0:T(8,128)(2,1)}, u32[]{:S(2)}) copy-start(bf16[32,32,1536]{2,1,0:T(8,128)(2,1)} %copy-done.1) | copy-start | bytes 9437188 | tf_op jit(solution)/shard_map/while
  166.4 6.4 %copy-start.1 = (bf16[32,32,1536]{2,1,0:T(8,128)(2,1)}, bf16[32,32,1536]{2,1,0:T(8,128)(2,1)S(1)}, u32[]{:S(2)}) copy-start(bf16[32,32,1536]{2,1,0:T(8,128)(2,1)S(1)} %get-tuple-element.215) | copy-start | bytes 9437188 | tf_op jit(solution)/shard_map/while
  187.1 9.9 %copy-start.2 = (bf16[32,32,1536]{2,1,0:T(8,128)(2,1)S(1)}, bf16[32,32,1536]{2,1,0:T(8,128)(2,1)}, u32[]{:S(2)}) copy-start(bf16[32,32,1536]{2,1,0:T(8,128)(2,1)} %copy-done.1) | copy-start | bytes 9437188 | tf_op jit(solution)/shard_map/while
  197.0 6.4 %copy-start.1 = (bf16[32,32,1536]{2,1,0:T(8,128)(2,1)}, bf16[32,32,1536]{2,1,0:T(8,128)(2,1)S(1)}, u32[]{:S(2)}) copy-start(bf16[32,32,1536]{2,1,0:T(8,128)(2,1)S(1)} %get-tuple-element.215) | copy-start | bytes 9437188 | tf_op jit(solution)/shard_map/while
  217.8 9.8 %copy-start.2 = (bf16[32,32,1536]{2,1,0:T(8,128)(2,1)S(1)}, bf16[32,32,1536]{2,1,0:T(8,128)(2,1)}, u32[]{:S(2)}) copy-start(bf16[32,32,1536]{2,1,0:T(8,128)(2,1)} %copy-done.1) | copy-start | bytes 9437188 | tf_op jit(solution)/shard_map/while
Sparse Core Ops, SparseCore 0:
  105.2 479.5 all-reduce.11
where the time goes:
time: 597 us; the launch traced here: 595 us
  waiting for transfers between devices  407 us (68%)
  local copies, waits for them, and re-layouts  93.3 us (16%)
  matrix products  46.1 us (8%)
  between operations  14.3 us (2%)
  other arithmetic  12.5 us (2%)
  starting transfers between devices  11.1 us (2%)
  loops' own time  10.9 us (2%)
    psum x1, waiting for transfers between devices, per_device(): grad_q, grad_k = lax.psum((grad_q, grad_k), ('img', 'py', 'px'))  355 us
    ppermute x2, waiting for transfers between devices, extended_2(): lax.ppermute(tail, axis, [(i, (i + 1) % count) for i in range(ends)])  42.4 us
    reshape x8, local copies, waits for them, and re-layouts, regroup(): return window.reshape(width, BS, width, BS, feat).transpose(0, 2, 1, 3, 4...  22.8 us
    dot_general x4, matrix products, one_block(): jnp.einsum('hqk,khd->qhd', probs, window_v, preferred_element_type=jnp.fl...  18.8 us
    transpose x8, local copies, waits for them, and re-layouts, regroup(): return window.reshape(width, BS, width, BS, feat).transpose(0, 2, 1, 3, 4...  12.4 us
    dynamic_slice x4, local copies, waits for them, and re-layouts, one_block(): lax.dynamic_slice(key_ext, (start_y, start_x, anchor), (side, side, feat))  12.2 us
  transfers between devices with their start and end apart: 5, of which 5 were waited for; matrix products, arithmetic and copies ran while one was open for 20% of the time, Pallas kernels for 0%

commit v1 on v0

--- a/solution.py
+++ b/solution.py
@@ -129,7 +129,7 @@
         )
 
     grad_q, grad_k = jax.grad(local_loss, argnums=(0, 1))(router_q, router_k)
-    grad_q, grad_k = lax.psum((grad_q, grad_k), ("img", "py", "px"))
+    grad_q, grad_k = lax.psum(lax.psum((grad_q, grad_k), ("py", "px")), "img")
     return (attended, grad_q, grad_k)
 
 

time: 597 us -> 646 us (1.082)
  the two profiles are of different devices: /device:TPU:2 before, /device:TPU:1 now
where the time goes in v1:
time: 646 us; the launch traced here: 644 us
  waiting for transfers between devices  452 us (70%)
  local copies, waits for them, and re-layouts  93.2 us (14%)
  matrix products  46.1 us (7%)
  starting transfers between devices  14.8 us (2%)
  between operations  14.3 us (2%)
  other arithmetic  12.5 us (2%)
  loops' own time  10.9 us (2%)
    psum x2, waiting for transfers between devices, per_device(): grad_q, grad_k = lax.psum(lax.psum((grad_q, grad_k), ('py', 'px')), 'img')  405 us
    ppermute x2, waiting for transfers between devices, extended_2(): lax.ppermute(tail, axis, [(i, (i + 1) % count) for i in range(ends)])  38.1 us
    reshape x8, local copies, waits for them, and re-layouts, regroup(): return window.reshape(width, BS, width, BS, feat).transpose(0, 2, 1, 3, 4...  22.8 us
    dot_general x4, matrix products, one_block(): jnp.einsum('hqk,khd->qhd', probs, window_v, preferred_element_type=jnp.fl...  18.8 us
  transfers between devices with their start and end apart: 6, of which 6 were waited for; matrix products, arithmetic and copies ran while one was open for 18% of the time, Pallas kernels for 0%

profile of v1, /device:TPU:1, one launch (start us, length us, event | category | flops | bytes accessed | tf_op | source)
XLA Modules:
  0.0 644.2 jit_solution(15841915333563884405)
XLA Ops:
  7.2 1.6 fusion.31
  8.9 4.1 collective-permute-start
  14.2 11.7 %collective-permute-done = bf16[2,1,8,16,1536]{4,3,2,1,0:T(8,128)(2,1)S(1)} collective-permute-done((bf16[2,1,8,16,1536]{4,3,2,1,0:T(8,128)(2,1)S(1)}, bf16[2,1,8,16,1536]{4,3,2,1,0:T(8,128)(2,1)S(1)}, u32[]{:S(2)}, u32[]{:S(2)}) %collective-permute-start) | collective-permute-done | bytes 786464 | tf_op jit(solution)/shard_map/ppermute | solution.py:24
  25.9 3.9 collective-permute-done.1
  31.2 1.9 fusion.85
  33.1 7.9 %collective-permute-start.2 = (bf16[2,1,32,8,1536]{4,3,2,1,0:T(8,128)(2,1)}, bf16[2,1,32,8,1536]{4,3,2,1,0:T(8,128)(2,1)}, u32[]{:S(2)}, u32[]{:S(2)}) collective-permute-start(bf16[2,1,32,8,1536]{4,3,2,1,0:T(8,128)(2,1)} %get-tuple-element.123), channel_id=1, source_target_pairs={{0,1},{1,2},{2,3},{4,5},{5,6},{6,7},{8,9},{9,10},{10,11},{12,13},{... | collective-permute-start | bytes 4718600 | tf_op jit(solution)/shard_map/ppermute | solution.py:24
  43.9 1.7 fusion.37
  45.6 26.4 %collective-permute-done.2 = bf16[2,1,32,8,1536]{4,3,2,1,0:T(8,128)(2,1)} collective-permute-done((bf16[2,1,32,8,1536]{4,3,2,1,0:T(8,128)(2,1)}, bf16[2,1,32,8,1536]{4,3,2,1,0:T(8,128)(2,1)}, u32[]{:S(2)}, u32[]{:S(2)}) %collective-permute-start.2) | collective-permute-done | bytes 1572896 | tf_op jit(solution)/shard_map/ppermute | solution.py:24
  72.0 5.0 collective-permute-done.3
  77.0 3.2 pad_maximum_fusion
  80.2 2.4 fusion.84
  92.3 1.6 copy.53
  98.7 2.3 convolution_bitcast_fusion
  101.0 2.6 convolution_bitcast_fusion.1
  103.9 169.9 %all-reduce.16.cloned.1.call-done = (f32[12,128,64]{1,2,0:T(8,128)}, f32[12,128,64]{1,2,0:T(8,128)}) async-done(((f32[12,128,64]{1,2,0:T(8,128)}, f32[12,128,64]{1,2,0:T(8,128)}), (f32[12,128,64]{1,2,0:T(8,128)}, f32[12,128,64]{1,2,0:T(8,128)})) %all-reduce.16.cloned.1.call-update) | async-done | bytes 786448 | tf_op jit(solution)/shard_map/psum | solution.py:132
  273.8 122.4 %while.12 = (s32[]{:T(128)}, bf16[4,8,8,1536]{3,2,1,0:T(8,128)(2,1)}, s32[4]{0:T(128)S(1)}, bf16[32,32,1536]{2,1,0:T(8,128)(2,1)}, s32[2,2,9]{2,1,0:T(2,128)S(1)...) while((s32[]{:T(128)}, ...), condition=%wide.region_3.4_spmd, body=%wide.region_0.3_spmd.sunk | while | flops 343820224 | bytes 57812960 | solution.py:75
  277.2 3.0 constant_dynamic-slice_fusion.6
  280.2 1.5 copy.118
  281.7 3.0 reshape.102
  285.8 2.2 fusion.101
  288.3 2.0 fusion.100
  290.3 1.6 copy.117
  291.9 2.7 reshape.101
  294.6 4.7 fusion.102
  299.3 1.8 copy.119
  301.0 1.8 broadcast_in_dim.131
  302.8 1.6 constant_dynamic-update-slice_fusion.2
  307.8 3.0 constant_dynamic-slice_fusion.6
  310.8 1.5 copy.118
  312.3 3.0 reshape.102
  316.4 2.2 fusion.101
  318.9 2.0 fusion.100
  320.9 1.6 copy.117
  322.5 2.7 reshape.101
  325.2 4.7 fusion.102
  329.9 1.8 copy.119
  331.6 1.8 broadcast_in_dim.131
  333.4 1.6 constant_dynamic-update-slice_fusion.2
  338.4 3.0 constant_dynamic-slice_fusion.6
  341.4 1.5 copy.118
  342.9 3.0 reshape.102
  347.0 2.2 fusion.101
  349.4 2.0 fusion.100
  351.5 1.6 copy.117
  353.1 2.7 reshape.101
  355.8 4.7 fusion.102
  360.5 1.8 copy.119
  362.2 1.8 broadcast_in_dim.131
  364.0 1.6 constant_dynamic-update-slice_fusion.2
  369.0 3.1 constant_dynamic-slice_fusion.6
  372.0 1.5 copy.118
  373.5 3.0 reshape.102
  377.7 2.2 fusion.101
  380.1 2.0 fusion.100
  382.1 1.6 copy.117
  383.7 2.7 reshape.101
  386.4 4.7 fusion.102
  391.1 1.8 copy.119
  392.9 1.8 broadcast_in_dim.131
  394.6 1.6 constant_dynamic-update-slice_fusion.2
  396.3 2.1 copy.48
  398.3 235.5 %all-reduce.14.cloned.1.call-done = (f32[12,128,64]{1,2,0:T(8,128)}, f32[12,128,64]{1,2,0:T(8,128)}) async-done(((f32[12,128,64]{1,2,0:T(8,128)}, f32[12,128,64]{1,2,0:T(8,128)}), (f32[12,128,64]{1,2,0:T(8,128)}, f32[12,128,64]{1,2,0:T(8,128)})) %all-reduce.14.cloned.1.call-update) | async-done | bytes 786448 | tf_op jit(solution)/shard_map/psum | solution.py:132
  633.8 1.8 copy.139
  635.6 1.8 copy.140
  (98 shorter events, 28.0 us)
Async XLA Ops:
  7.2 76.7 %copy-start = (f32[12,128,64]{1,2,0:T(8,128)S(1)}, f32[12,128,64]{1,2,0:T(8,128)}, u32[]{:S(2)}) copy-start(f32[12,128,64]{1,2,0:T(8,128)} %param.15) | copy-start | bytes 1179652
  7.2 23.5 %copy-start.3 = (bf16[1,16,16,1536]{3,2,1,0:T(8,128)(2,1)S(1)}, bf16[1,16,16,1536]{3,2,1,0:T(8,128)(2,1)}, u32[]{:S(2)}) copy-start(bf16[1,16,16,1536]{3,2,1,0:T(8,128)(2,1)} %param.10) | copy-start | bytes 2359300
  7.2 23.5 %copy-start.4 = (bf16[1,16,16,1536]{3,2,1,0:T(8,128)(2,1)S(1)}, bf16[1,16,16,1536]{3,2,1,0:T(8,128)(2,1)}, u32[]{:S(2)}) copy-start(bf16[1,16,16,1536]{3,2,1,0:T(8,128)(2,1)} %param.11) | copy-start | bytes 2359300
  7.2 266.6 %all-reduce.16.cloned.1.call-start = ((), (), s32[]{:S(2)}) async-start(), calls=%async_computation.1 | async-start | bytes 1572864 | tf_op jit(solution)/shard_map/psum | solution.py:132
  8.9 17.1 %collective-permute-start = (bf16[2,1,8,16,1536]{4,3,2,1,0:T(8,128)(2,1)S(1)}, bf16[2,1,8,16,1536]{4,3,2,1,0:T(8,128)(2,1)S(1)}, u32[]{:S(2)}, u32[]{:S(2)}) collective-permute-start(bf16[2,1,8,16,1536]{4,3,2,1,0:T(8,128)(2,1)S(1)} %get-tuple-element.125), channel_id=1, source_target_pairs={{0,4},{4,8},{8,12},{1,5},{5,9},{9,13},{2,6},{6,10},{10,14},{3,7},{... | collective-permute-start | bytes 2359304 | tf_op jit(solution)/shard_map/ppermute | solution.py:24
  12.9 16.9 %collective-permute-start.1 = (bf16[2,1,8,16,1536]{4,3,2,1,0:T(8,128)(2,1)S(1)}, bf16[2,1,8,16,1536]{4,3,2,1,0:T(8,128)(2,1)S(1)}, u32[]{:S(2)}, u32[]{:S(2)}) collective-permute-start(bf16[2,1,8,16,1536]{4,3,2,1,0:T(8,128)(2,1)S(1)} %get-tuple-element.126), channel_id=1, source_target_pairs={{4,0},{8,4},{12,8},{5,1},{9,5},{13,9},{6,2},{10,6},{14,10},{7,3},{... | collective-permute-start | bytes 2359304 | tf_op jit(solution)/shard_map/ppermute | solution.py:26
  29.8 0.9 copy-start.6
  31.1 11.1 %copy-start.11 = (s32[1,2,2,9]{3,2,1,0:T(2,128)S(1)}, s32[1,2,2,9]{3,2,1,0:T(2,128)}, u32[]{:S(2)}) copy-start(s32[1,2,2,9]{3,2,1,0:T(2,128)} %param.12) | copy-start | bytes 436
  31.1 12.6 %copy-start.5 = (bf16[1,16,16,1536]{3,2,1,0:T(8,128)(2,1)S(1)}, bf16[1,16,16,1536]{3,2,1,0:T(8,128)(2,1)}, u32[]{:S(2)}) copy-start(bf16[1,16,16,1536]{3,2,1,0:T(8,128)(2,1)} %param.9) | copy-start | bytes 2359300
  33.1 38.9 %collective-permute-start.2 = (bf16[2,1,32,8,1536]{4,3,2,1,0:T(8,128)(2,1)}, bf16[2,1,32,8,1536]{4,3,2,1,0:T(8,128)(2,1)}, u32[]{:S(2)}, u32[]{:S(2)}) collective-permute-start(bf16[2,1,32,8,1536]{4,3,2,1,0:T(8,128)(2,1)} %get-tuple-element.123), channel_id=1, source_target_pairs={{0,1},{1,2},{2,3},{4,5},{5,6},{6,7},{8,9},{9,10},{10,11},{12,13},{... | collective-permute-start | bytes 4718600 | tf_op jit(solution)/shard_map/ppermute | solution.py:24
  40.9 36.1 %collective-permute-start.3 = (bf16[2,1,32,8,1536]{4,3,2,1,0:T(8,128)(2,1)}, bf16[2,1,32,8,1536]{4,3,2,1,0:T(8,128)(2,1)}, u32[]{:S(2)}, u32[]{:S(2)}) collective-permute-start(bf16[2,1,32,8,1536]{4,3,2,1,0:T(8,128)(2,1)} %get-tuple-element.124), channel_id=1, source_target_pairs={{1,0},{2,1},{3,2},{5,4},{6,5},{7,6},{9,8},{10,9},{11,10},{13,12},{... | collective-permute-start | bytes 4718600 | tf_op jit(solution)/shard_map/ppermute | solution.py:26
  43.9 33.1 %copy-start.10 = (f32[2,2,12,128]{3,2,1,0:T(8,128)}, f32[2,2,12,128]{3,2,1,0:T(8,128)S(1)}, u32[]{:S(2)}) copy-start(f32[2,2,12,128]{3,2,1,0:T(8,128)S(1)} %broadcast_multiply_fusion.1) | copy-start | bytes 73732
  45.6 39.2 %copy-start.9 = (f32[12,2,2,64]{3,2,1,0:T(2,128)}, f32[12,2,2,64]{3,2,1,0:T(2,128)S(1)}, u32[]{:S(2)}) copy-start(f32[12,2,2,64]{3,2,1,0:T(2,128)S(1)} %fusion.37) | copy-start | bytes 36868
  83.2 0.7 copy-start.8
  84.9 0.7 copy-start.7
  103.7 530.2 %all-reduce.14.cloned.1.call-start = ((), (), s32[]{:S(2)}) async-start(), calls=%async_computation | async-start | bytes 1572864 | tf_op jit(solution)/shard_map/psum | solution.py:132
  273.9 6.4 copy-start.1
  294.6 9.9 %copy-start.2 = (bf16[32,32,1536]{2,1,0:T(8,128)(2,1)S(1)}, bf16[32,32,1536]{2,1,0:T(8,128)(2,1)}, u32[]{:S(2)}) copy-start(bf16[32,32,1536]{2,1,0:T(8,128)(2,1)} %copy-done.1) | copy-start | bytes 9437188 | tf_op jit(solution)/shard_map/while
  304.4 6.4 copy-start.1
  325.2 9.9 %copy-start.2 = (bf16[32,32,1536]{2,1,0:T(8,128)(2,1)S(1)}, bf16[32,32,1536]{2,1,0:T(8,128)(2,1)}, u32[]{:S(2)}) copy-start(bf16[32,32,1536]{2,1,0:T(8,128)(2,1)} %copy-done.1) | copy-start | bytes 9437188 | tf_op jit(solution)/shard_map/while
  335.0 6.4 copy-start.1
  355.8 9.9 %copy-start.2 = (bf16[32,32,1536]{2,1,0:T(8,128)(2,1)S(1)}, bf16[32,32,1536]{2,1,0:T(8,128)(2,1)}, u32[]{:S(2)}) copy-start(bf16[32,32,1536]{2,1,0:T(8,128)(2,1)} %copy-done.1) | copy-start | bytes 9437188 | tf_op jit(solution)/shard_map/while
  365.6 6.4 copy-start.1
  386.4 9.8 %copy-start.2 = (bf16[32,32,1536]{2,1,0:T(8,128)(2,1)S(1)}, bf16[32,32,1536]{2,1,0:T(8,128)(2,1)}, u32[]{:S(2)}) copy-start(bf16[32,32,1536]{2,1,0:T(8,128)(2,1)} %copy-done.1) | copy-start | bytes 9437188 | tf_op jit(solution)/shard_map/while
Sparse Core Ops, SparseCore 0:
  103.8 169.9 all-reduce.15
  276.7 357.0 all-reduce.13
